TPU v7x, 32 devices: a whole 2x2x4 slice. The times are simulated.
32 devices in a mesh: groups: 2 (over y), seq: 16 (over z, x, core).
Axes of the slice: x: 2, y: 2, z: 4, core: 2. Of those that a mesh axis runs over, the one named last changes fastest.
Arguments:
- residual: bfloat16 [8192, 1024], P(('groups', 'seq')), parts along dimension 0, may hold values from -6 to 6
- layer_queries: bfloat16 [8192, 512], P(('groups', 'seq')), parts along dimension 0, may hold values from -200 to 200
- layer_keyvals: bfloat16 [8192, 256], P(('groups', 'seq')), parts along dimension 0, may hold values from -8 to 8
- head_window_extent: int32 [8], replicated, may hold values from 32 to 256, as said below
- block_mask: int32 [16, 4], P('seq'), may hold values 0 or 1
- first_out: bfloat16 [512, 1024], replicated, may hold values from -1 to 1
- second_query: bfloat16 [1024, 512], replicated, may hold values from -12 to 12
- second_keyval: bfloat16 [1024, 256], replicated, may hold values from -1 to 1
- second_out: bfloat16 [512, 1024], replicated, may hold values from -1 to 1
Outputs:
- layer_output: bfloat16 [8192, 1024], P(('groups', 'seq')), parts along dimension 0
There are 2 independent parts, one for each index of `groups`. A program takes and returns all parts, laid end to end along the dimension named above; an argument that names none is the same for every part. Nothing has to cross between parts.
Inputs may be any that keep to these rules, and one draw needn't show every extreme that they name: `head_window_extent`: per head; some head has exactly 256 and some exactly 32.
All inputs are finite; a program needn't handle non-finite values. No bound on the sum of `block_mask` on one device may be relied on, other than what follows from the above.
Results may differ from a plain program's by a relative error of at most 0.0065.
Values may be sent and summed in bfloat16 or wider, within the bound.
A program may use at most 64 MiB of HBM per device.

v0:
```python
import jax
import jax.numpy as jnp
from jax import lax
from jax.sharding import PartitionSpec as P

QUERY_HEADS = 8
HEAD_SIZE = 64
WIN = 256


def with_halo(cells, sides, width):
    for axis, dim in sides:
        count = lax.axis_size(axis)
        ends = count - 1
        head = lax.slice_in_dim(cells, 0, width, axis=dim)
        tail = lax.slice_in_dim(cells, cells.shape[dim] - width, cells.shape[dim], axis=dim)
        cells = jnp.concatenate(
            [
                lax.ppermute(tail, axis, [(i, (i + 1) % count) for i in range(ends)]),
                cells,
                lax.ppermute(head, axis, [((i + 1) % count, i) for i in range(ends)]),
            ],
            axis=dim,
        )
    return cells


def swapped(block, axis, stride):
    count = lax.axis_size(axis)
    route = []
    for low in range(count):
        high = low | 1 << stride
        if high != low and high < count:
            route += [(low, high), (high, low)]
    return lax.ppermute(block, axis, route)


def norm_rows(hidden):
    values = hidden.astype(jnp.float32)
    scale = lax.rsqrt(jnp.mean(values * values, axis=-1, keepdims=True) + 1e-05)
    return (values * scale).astype(jnp.bfloat16)


def attend_rows(query_matrix, key_row_matrix, value_row_matrix, allowed):
    count_of_rows = query_matrix.shape[0]
    count_of_keys = key_row_matrix.shape[0]
    kv_heads = key_row_matrix.shape[1] // HEAD_SIZE
    heads_per_group = query_matrix.shape[1] // (kv_heads * HEAD_SIZE)
    query_head_rows = query_matrix.reshape(count_of_rows, kv_heads, heads_per_group, HEAD_SIZE)
    key_head_rows = key_row_matrix.reshape(count_of_keys, kv_heads, HEAD_SIZE)
    value_head_rows = value_row_matrix.reshape(count_of_keys, kv_heads, HEAD_SIZE)
    scores = jnp.einsum(
        "rkgd,jkd->kgrj", query_head_rows, key_head_rows, preferred_element_type=jnp.float32
    ) * HEAD_SIZE ** (-0.5)
    scores = jnp.where(allowed, scores, -1e30)
    row_max = jnp.max(scores, axis=-1, keepdims=True)
    weights = jnp.where(allowed, jnp.exp(scores - row_max), 0.0)
    shares = (weights / jnp.sum(weights, axis=-1, keepdims=True)).astype(jnp.bfloat16)
    mixture = jnp.einsum(
        "kgrj,jkd->rkgd", shares, value_head_rows, preferred_element_type=jnp.float32
    )
    return mixture.reshape(count_of_rows, query_matrix.shape[1]).astype(jnp.bfloat16)


def attend_groups(query_matrix, key_row_matrix, value_row_matrix, key_allowed):
    count_of_rows = query_matrix.shape[0]
    count_of_keys = key_row_matrix.shape[0]
    kv_heads = key_row_matrix.shape[1] // HEAD_SIZE
    heads_per_group = query_matrix.shape[1] // (kv_heads * HEAD_SIZE)
    query_head_rows = jnp.moveaxis(
        query_matrix.reshape(count_of_rows, kv_heads, heads_per_group, HEAD_SIZE), 2, 0
    )
    key_head_rows = key_row_matrix.reshape(count_of_keys, kv_heads, HEAD_SIZE)
    value_head_rows = value_row_matrix.reshape(count_of_keys, kv_heads, HEAD_SIZE)
    allowed = key_allowed[None, None, :]

    def one_group(q_group):
        scores = jnp.einsum(
            "rkd,jkd->krj", q_group, key_head_rows, preferred_element_type=jnp.float32
        ) * HEAD_SIZE ** (-0.5)
        scores = jnp.where(allowed, scores, -1e30)
        row_max = jnp.max(scores, axis=-1, keepdims=True)
        weights = jnp.where(allowed, jnp.exp(scores - row_max), 0.0)
        shares = (weights / jnp.sum(weights, axis=-1, keepdims=True)).astype(jnp.bfloat16)
        return jnp.einsum(
            "krj,jkd->rkd", shares, value_head_rows, preferred_element_type=jnp.float32
        ).astype(jnp.bfloat16)

    mixture = lax.map(one_group, query_head_rows)
    return jnp.moveaxis(mixture, 0, 2).reshape(count_of_rows, query_matrix.shape[1])


def shards(
    residual,
    layer_queries,
    layer_keyvals,
    head_window_extent,
    block_mask,
    first_out,
    second_query,
    second_keyval,
    second_out,
):
    local_rows = residual.shape[0]
    key_value_width = layer_keyvals.shape[1] // 2
    kv_heads = key_value_width // HEAD_SIZE
    heads_per_group = QUERY_HEADS // kv_heads
    block_rows = min(local_rows, 512)
    block_count = local_rows // block_rows
    extended = with_halo(layer_keyvals, (("seq", 0),), WIN)
    start_row = lax.axis_index("seq") * local_rows
    total_rows = lax.axis_size("seq") * local_rows
    window_extent = head_window_extent.reshape(kv_heads, heads_per_group, 1, 1)

    def window_block(block_index):
        first_row = block_index * block_rows
        query_pos = start_row + first_row + jnp.arange(block_rows, dtype=jnp.int32)
        key_pos = start_row - WIN + first_row + jnp.arange(block_rows + 2 * WIN, dtype=jnp.int32)
        inside = (key_pos >= 0) & (key_pos < total_rows)
        distance = jnp.abs(query_pos[:, None] - key_pos[None, :])
        allowed = (distance[None, None] <= window_extent) & inside[None, None, None, :]
        return attend_rows(
            layer_queries, extended[:, :key_value_width], extended[:, key_value_width:], allowed
        )

    attended = lax.map(window_block, jnp.arange(block_count, dtype=jnp.int32)).reshape(
        local_rows, -1
    )
    hidden = (
        jnp.dot(attended, first_out, preferred_element_type=jnp.float32)
        + residual.astype(jnp.float32)
    ).astype(jnp.bfloat16)
    normed = norm_rows(hidden)
    queries_two = jnp.dot(normed, second_query, preferred_element_type=jnp.float32).astype(
        jnp.bfloat16
    )
    keyvals_two = jnp.dot(normed, second_keyval, preferred_element_type=jnp.float32).astype(
        jnp.bfloat16
    )
    level_count = lax.axis_size("seq").bit_length() - 1
    levels = list(range(level_count))
    key_blocks = [keyvals_two]
    key_flags = [jnp.ones((), jnp.bool_)]
    for level in levels:
        key_blocks.append(swapped(keyvals_two, "seq", level))
        key_flags.append(block_mask[0, level] == 1)
    all_keys = jnp.concatenate(key_blocks, axis=0)
    key_allowed = jnp.repeat(jnp.stack(key_flags), local_rows)

    def butterfly_block(block_index):
        return attend_groups(
            queries_two, all_keys[:, :key_value_width], all_keys[:, key_value_width:], key_allowed
        )

    second = lax.map(butterfly_block, jnp.arange(block_count, dtype=jnp.int32)).reshape(
        local_rows, -1
    )
    output = jnp.dot(second, second_out, preferred_element_type=jnp.float32) + hidden.astype(
        jnp.float32
    )
    return output.astype(jnp.bfloat16)


def solution(mesh):
    placed = (
        P(("groups", "seq"), None),
        P(("groups", "seq"), None),
        P(("groups", "seq"), None),
        P(),
        P("seq", None),
        P(),
        P(),
        P(),
        P(),
    )
    return jax.shard_map(
        shards, mesh=mesh, in_specs=placed, out_specs=P(("groups", "seq"), None), check_vma=False
    )
```

profile of v0, /device:TPU:0, one launch (start us, length us, event | category | flops | bytes accessed | tf_op | source)
XLA Modules:
  0.0 63.5 jit_solution(9689028794966576870)
XLA Ops:
  0.0 0.0 copy-start
  0.0 2.5 %collective-permute-start = (bf16[256,256]{1,0:T(8,128)(2,1)}, bf16[256,256]{1,0:T(8,128)(2,1)S(1)}, u32[]{:S(2)}, u32[]{:S(2)}) collective-permute-start(bf16[256,256]{1,0:T(8,128)(2,1)} %param.13), channel_id=1, source_target_pairs={{0,1},{1,2},{2,3},{3,4},{4,5},{5,6},{6,7},{7,8},{8,9},{9,10},{10,1... | collective-permute-start | bytes 393224 | tf_op jit(solution)/shard_map/ppermute | solution.py:19
  2.5 1.3 %collective-permute-start.1 = (bf16[256,256]{1,0:T(8,128)(2,1)}, bf16[256,256]{1,0:T(8,128)(2,1)S(1)}, u32[]{:S(2)}, u32[]{:S(2)}) collective-permute-start(bf16[256,256]{1,0:T(8,128)(2,1)} %param.13), channel_id=1, source_target_pairs={{1,0},{2,1},{3,2},{4,3},{5,4},{6,5},{7,6},{8,7},{9,8},{10,9},{11,1... | collective-permute-start | bytes 393224 | tf_op jit(solution)/shard_map/ppermute | solution.py:21
  3.9 0.2 subtract_abs_fusion
  4.0 1.5 %fusion.49 = (s32[1,1]{1,0:T(1,128)}, s32[1,1]{1,0:T(1,128)}, s32[1,1]{1,0:T(1,128)}, s32[1,1]{1,0:T(1,128)}) fusion(s32[1,4]{1,0:T(1,128)} %param.15), kind=kLoop, calls=%fused_computation.63 | loop fusion | bytes 32 | tf_op jit(solution)/shard_map/slice | solution.py:146
  5.5 0.7 %le.23 = s32[2,4]{1,0:T(2,128)S(1)} reshape(s32[8]{0:T(128)} %param.14) | data formatting | bytes 64 | tf_op jit(solution)/shard_map/while/body/eval_jaxpr/le | solution.py:121
  6.3 1.1 %copy.19 = bf16[256,512]{0,1:T(8,128)(2,1)S(1)} copy(bf16[256,512]{1,0:T(8,128)(2,1)} %param.12) | data formatting | bytes 524288 | tf_op args[1]
  9.9 0.1 stack.19
  10.0 0.0 collective-permute-done
  10.0 0.9 %constant_dynamic-update-slice_fusion.1 = bf16[768,256]{1,0:T(8,128)(2,1)S(1)} fusion(bf16[768,256]{1,0:T(8,128)(2,1)S(1)} %constant_dynamic-update-slice_fusion.2, bf16[256,256]{1,0:T(8,128)(2,1)} %param.13), kind=kLoop, calls=%fused_computation.47 | loop fusion | bytes 262144
  10.9 0.0 collective-permute-done.1
  11.0 0.1 copy.17
  11.1 0.1 copy.18
  11.3 6.6 %fusion.50 = (f32[2,4,256]{2,1,0:T(4,128)S(1)}, f32[2,4,256,768]{2,3,1,0:T(8,128)}) fusion(s32[2,4]{1,0:T(2,128)S(1)} %le.23, s32[256,768]{0,1:T(8,128)S(1)} %subtract_abs_fusion, pred[768]{0:T(1024)(128)(4,1)S(1)} %compare_and_fusion.1, bf16[768,2,64,1]{0,2,3,1:T(8,128)(2,1)S(1)} %bitcast.78, bf16[256,2,4,64]{0,3,2,1:T(8,128)(2,1)S(1)} %bitcast.76), kind=kOutput, calls=%fused_computation.64 | convolution fusion | flops 215483136 | bytes 7545632 | tf_op jit(solution)/shard_map/while/body/eval_jaxpr/sub | solution.py:57
  17.9 0.0 copy-start.3
  17.9 3.5 %fusion.35 = bf16[2,64,4,256]{3,1,2,0:T(8,128)(2,1)S(1)} fusion(bf16[768,2,64,1]{0,2,3,1:T(8,128)(2,1)S(1)} %bitcast.77, f32[2,4,256,768]{2,3,1,0:T(8,128)} %get-tuple-element.121, f32[2,4,256]{2,1,0:T(4,128)S(1)} %get-tuple-element.120), kind=kOutput, calls=%fused_computation.39 | convolution fusion | flops 204603392 | bytes 6758400 | tf_op jit(solution)/shard_map/while/body/eval_jaxpr/kgrj,jkd->rkgd/dot_general | solution.py:59
  21.4 0.0 copy-start.4
  21.5 0.0 copy-start.2
  21.5 0.0 copy-done
  21.5 0.0 copy-done.3
  21.5 0.6 fusion.36
  22.1 0.4 copy-done.4
  22.5 0.4 constant_dynamic-update-slice_fusion.7
  22.8 3.3 %collective-permute-start.2 = (bf16[256,256]{1,0:T(8,128)(2,1)S(1)}, bf16[256,256]{1,0:T(8,128)(2,1)S(1)}, u32[]{:S(2)}, u32[]{:S(2)}) collective-permute-start(bf16[256,256]{1,0:T(8,128)(2,1)S(1)} %get-tuple-element.125), channel_id=1, source_target_pairs={{0,1},{1,0},{2,3},{3,2},{4,5},{5,4},{6,7},{7,6},{8,9},{9,8},{10,11... | collective-permute-start | bytes 393224 | tf_op jit(solution)/shard_map/ppermute | solution.py:35
  26.1 1.7 %collective-permute-start.3 = (bf16[256,256]{1,0:T(8,128)(2,1)S(1)}, bf16[256,256]{1,0:T(8,128)(2,1)S(1)}, u32[]{:S(2)}, u32[]{:S(2)}) collective-permute-start(bf16[256,256]{1,0:T(8,128)(2,1)S(1)} %get-tuple-element.125), channel_id=1, source_target_pairs={{0,2},{2,0},{1,3},{3,1},{4,6},{6,4},{5,7},{7,5},{8,10},{10,8},{9,1... | collective-permute-start | bytes 393224 | tf_op jit(solution)/shard_map/ppermute | solution.py:35
  27.8 1.6 %collective-permute-start.4 = (bf16[256,256]{1,0:T(8,128)(2,1)S(1)}, bf16[256,256]{1,0:T(8,128)(2,1)S(1)}, u32[]{:S(2)}, u32[]{:S(2)}) collective-permute-start(bf16[256,256]{1,0:T(8,128)(2,1)S(1)} %get-tuple-element.125), channel_id=1, source_target_pairs={{0,4},{4,0},{1,5},{5,1},{2,6},{6,2},{3,7},{7,3},{8,12},{12,8},{9,1... | collective-permute-start | bytes 393224 | tf_op jit(solution)/shard_map/ppermute | solution.py:35
  29.4 2.6 %collective-permute-start.5 = (bf16[256,256]{1,0:T(8,128)(2,1)S(1)}, bf16[256,256]{1,0:T(8,128)(2,1)S(1)}, u32[]{:S(2)}, u32[]{:S(2)}) collective-permute-start(bf16[256,256]{1,0:T(8,128)(2,1)S(1)} %get-tuple-element.125), channel_id=1, source_target_pairs={{0,8},{8,0},{1,9},{9,1},{2,10},{10,2},{3,11},{11,3},{4,12},{12,4},... | collective-permute-start | bytes 393224 | tf_op jit(solution)/shard_map/ppermute | solution.py:35
  32.0 0.0 copy-done.2
  32.0 0.5 convolution_convert_fusion
  32.5 0.8 %copy.21 = bf16[256,512]{0,1:T(8,128)(2,1)} copy(bf16[256,512]{1,0:T(8,128)(2,1)S(1)} %convolution_convert_fusion) | data formatting | bytes 524288 | tf_op jit(solution)/shard_map/convert_element_type | solution.py:134
  33.3 0.0 collective-permute-done.2
  33.3 0.0 collective-permute-done.3
  33.4 2.3 %collective-permute-done.4 = bf16[256,256]{1,0:T(8,128)(2,1)S(1)} collective-permute-done((bf16[256,256]{1,0:T(8,128)(2,1)S(1)}, bf16[256,256]{1,0:T(8,128)(2,1)S(1)}, u32[]{:S(2)}, u32[]{:S(2)}) %collective-permute-start.4) | collective-permute-done | bytes 131104 | tf_op jit(solution)/shard_map/ppermute | solution.py:35
  35.7 2.7 %collective-permute-done.5 = bf16[256,256]{1,0:T(8,128)(2,1)S(1)} collective-permute-done((bf16[256,256]{1,0:T(8,128)(2,1)S(1)}, bf16[256,256]{1,0:T(8,128)(2,1)S(1)}, u32[]{:S(2)}, u32[]{:S(2)}) %collective-permute-start.5) | collective-permute-done | bytes 131104 | tf_op jit(solution)/shard_map/ppermute | solution.py:35
  38.5 0.2 copy.22
  38.7 0.2 copy.23
  38.9 0.0 copy-start.1
  38.9 23.3 %while.14 = (s32[]{:T(128)}, bf16[4,256,2,64]{1,3,0,2:T(8,128)(2,1)S(1)}, bf16[4,256,2,64]{1,3,0,2:T(8,128)(2,1)}, bf16[1280,2,64]{0,2,1:T(8,128)(2,1)S(1)}, bf1...) while((s32[]{:T(128)}, bf16[4,256,2,64]{1,3,0,2:T(8,128)(2,1)S(1)}, ...), condition=%wide.region_6.7_spmd.clone, body=%wide.region_3.6_spmd.clone.sunk | while | flops 172393728 | bytes 6041442 | solution.py:89
  38.9 0.1 broadcast_in_dim.98
  39.0 3.5 %fusion.70 = (f32[2,256]{1,0:T(2,128)S(1)}, f32[2,256,1280]{2,1,0:T(8,128)}) fusion(bf16[1280,2,64]{0,2,1:T(8,128)(2,1)S(1)} %get-tuple-element.184, pred[1280]{0:T(1024)(128)(4,1)S(1)} %broadcast_in_dim.99, bf16[4,256,2,64]{1,3,0,2:T(8,128)(2,1)} %get-tuple-element.183, s32[]{:T(128)S(6)} %copy.41), kind=kOutput, calls=%fused_computation.60.clone.1 | convolution fusion | flops 87164160 | bytes 3020804 | tf_op jit(solution)/shard_map/while/body/eval_jaxpr/while/body/eval_jaxpr/sub | solution.py:83
  42.4 2.3 %fusion.71 = bf16[4,256,2,64]{1,3,0,2:T(8,128)(2,1)S(1)} fusion(bf16[4,256,2,64]{1,3,0,2:T(8,128)(2,1)S(1)} %get-tuple-element.175, s32[]{:T(128)S(6)} %copy.41, bf16[1280,2,64]{0,2,1:T(8,128)(2,1)S(1)} %get-tuple-element.185, f32[2,256,1280]{2,1,0:T(8,128)} %get-tuple-element.165, f32[2,256]{1,0:T(2,128)S(1)} %get-tuple-element.166), kind=kOutput, calls=%fused_computation.11.clone.1 | convolution fusion | flops 85229568 | bytes 3016708 | tf_op jit(solution)/shard_map/while/body/eval_jaxpr/while/body/eval_jaxpr/krj,jkd->rkd/dot_general | solution.py:85
  44.8 0.1 broadcast_in_dim.98
  44.9 3.4 %fusion.70 = (f32[2,256]{1,0:T(2,128)S(1)}, f32[2,256,1280]{2,1,0:T(8,128)}) fusion(bf16[1280,2,64]{0,2,1:T(8,128)(2,1)S(1)} %get-tuple-element.184, pred[1280]{0:T(1024)(128)(4,1)S(1)} %broadcast_in_dim.99, bf16[4,256,2,64]{1,3,0,2:T(8,128)(2,1)} %get-tuple-element.183, s32[]{:T(128)S(6)} %copy.41), kind=kOutput, calls=%fused_computation.60.clone.1 | convolution fusion | flops 87164160 | bytes 3020804 | tf_op jit(solution)/shard_map/while/body/eval_jaxpr/while/body/eval_jaxpr/sub | solution.py:83
  48.2 2.3 %fusion.71 = bf16[4,256,2,64]{1,3,0,2:T(8,128)(2,1)S(1)} fusion(bf16[4,256,2,64]{1,3,0,2:T(8,128)(2,1)S(1)} %get-tuple-element.175, s32[]{:T(128)S(6)} %copy.41, bf16[1280,2,64]{0,2,1:T(8,128)(2,1)S(1)} %get-tuple-element.185, f32[2,256,1280]{2,1,0:T(8,128)} %get-tuple-element.165, f32[2,256]{1,0:T(2,128)S(1)} %get-tuple-element.166), kind=kOutput, calls=%fused_computation.11.clone.1 | convolution fusion | flops 85229568 | bytes 3016708 | tf_op jit(solution)/shard_map/while/body/eval_jaxpr/while/body/eval_jaxpr/krj,jkd->rkd/dot_general | solution.py:85
  50.6 0.1 broadcast_in_dim.98
  50.7 3.4 %fusion.70 = (f32[2,256]{1,0:T(2,128)S(1)}, f32[2,256,1280]{2,1,0:T(8,128)}) fusion(bf16[1280,2,64]{0,2,1:T(8,128)(2,1)S(1)} %get-tuple-element.184, pred[1280]{0:T(1024)(128)(4,1)S(1)} %broadcast_in_dim.99, bf16[4,256,2,64]{1,3,0,2:T(8,128)(2,1)} %get-tuple-element.183, s32[]{:T(128)S(6)} %copy.41), kind=kOutput, calls=%fused_computation.60.clone.1 | convolution fusion | flops 87164160 | bytes 3020804 | tf_op jit(solution)/shard_map/while/body/eval_jaxpr/while/body/eval_jaxpr/sub | solution.py:83
  54.1 2.3 %fusion.71 = bf16[4,256,2,64]{1,3,0,2:T(8,128)(2,1)S(1)} fusion(bf16[4,256,2,64]{1,3,0,2:T(8,128)(2,1)S(1)} %get-tuple-element.175, s32[]{:T(128)S(6)} %copy.41, bf16[1280,2,64]{0,2,1:T(8,128)(2,1)S(1)} %get-tuple-element.185, f32[2,256,1280]{2,1,0:T(8,128)} %get-tuple-element.165, f32[2,256]{1,0:T(2,128)S(1)} %get-tuple-element.166), kind=kOutput, calls=%fused_computation.11.clone.1 | convolution fusion | flops 85229568 | bytes 3016708 | tf_op jit(solution)/shard_map/while/body/eval_jaxpr/while/body/eval_jaxpr/krj,jkd->rkd/dot_general | solution.py:85
  56.4 0.1 broadcast_in_dim.98
  56.5 3.4 %fusion.70 = (f32[2,256]{1,0:T(2,128)S(1)}, f32[2,256,1280]{2,1,0:T(8,128)}) fusion(bf16[1280,2,64]{0,2,1:T(8,128)(2,1)S(1)} %get-tuple-element.184, pred[1280]{0:T(1024)(128)(4,1)S(1)} %broadcast_in_dim.99, bf16[4,256,2,64]{1,3,0,2:T(8,128)(2,1)} %get-tuple-element.183, s32[]{:T(128)S(6)} %copy.41), kind=kOutput, calls=%fused_computation.60.clone.1 | convolution fusion | flops 87164160 | bytes 3020804 | tf_op jit(solution)/shard_map/while/body/eval_jaxpr/while/body/eval_jaxpr/sub | solution.py:83
  59.9 2.3 %fusion.71 = bf16[4,256,2,64]{1,3,0,2:T(8,128)(2,1)S(1)} fusion(bf16[4,256,2,64]{1,3,0,2:T(8,128)(2,1)S(1)} %get-tuple-element.175, s32[]{:T(128)S(6)} %copy.41, bf16[1280,2,64]{0,2,1:T(8,128)(2,1)S(1)} %get-tuple-element.185, f32[2,256,1280]{2,1,0:T(8,128)} %get-tuple-element.165, f32[2,256]{1,0:T(2,128)S(1)} %get-tuple-element.166), kind=kOutput, calls=%fused_computation.11.clone.1 | convolution fusion | flops 85229568 | bytes 3016708 | tf_op jit(solution)/shard_map/while/body/eval_jaxpr/while/body/eval_jaxpr/krj,jkd->rkd/dot_general | solution.py:85
  62.2 0.0 copy-done.1
  62.2 1.3 %fusion.34 = bf16[256,1024]{1,0:T(8,128)(2,1)} fusion(bf16[256,1024]{1,0:T(8,128)(2,1)S(1)} %get-tuple-element.123, bf16[256,512]{0,1:T(8,128)(2,1)S(1)} %bitcast.74, bf16[512,1024]{1,0:T(8,128)(2,1)S(1)} %copy-done.1), kind=kOutput, calls=%fused_computation.38 | convolution fusion | flops 269221888 | bytes 2359296 | tf_op jit(solution)/shard_map/dot_general | solution.py:158
  (17 shorter events, 0.2 us)
Async XLA Ops:
  0.0 21.5 %copy-start = (bf16[512,1024]{1,0:T(8,128)(2,1)S(1)}, bf16[512,1024]{1,0:T(8,128)(2,1)}, u32[]{:S(2)}) copy-start(bf16[512,1024]{1,0:T(8,128)(2,1)} %param.16) | copy-start | bytes 3145732
  0.0 10.0 %collective-permute-start = (bf16[256,256]{1,0:T(8,128)(2,1)}, bf16[256,256]{1,0:T(8,128)(2,1)S(1)}, u32[]{:S(2)}, u32[]{:S(2)}) collective-permute-start(bf16[256,256]{1,0:T(8,128)(2,1)} %param.13), channel_id=1, source_target_pairs={{0,1},{1,2},{2,3},{3,4},{4,5},{5,6},{6,7},{7,8},{8,9},{9,10},{10,1... | collective-permute-start | bytes 393224 | tf_op jit(solution)/shard_map/ppermute | solution.py:19
  2.5 8.4 %collective-permute-start.1 = (bf16[256,256]{1,0:T(8,128)(2,1)}, bf16[256,256]{1,0:T(8,128)(2,1)S(1)}, u32[]{:S(2)}, u32[]{:S(2)}) collective-permute-start(bf16[256,256]{1,0:T(8,128)(2,1)} %param.13), channel_id=1, source_target_pairs={{1,0},{2,1},{3,2},{4,3},{5,4},{6,5},{7,6},{8,7},{9,8},{10,9},{11,1... | collective-permute-start | bytes 393224 | tf_op jit(solution)/shard_map/ppermute | solution.py:21
  17.9 3.6 %copy-start.3 = (bf16[256,1024]{1,0:T(8,128)(2,1)S(1)}, bf16[256,1024]{1,0:T(8,128)(2,1)}, u32[]{:S(2)}) copy-start(bf16[256,1024]{1,0:T(8,128)(2,1)} %param.11) | copy-start | bytes 1572868
  21.4 1.0 %copy-start.4 = (bf16[1024,256]{1,0:T(8,128)(2,1)S(1)}, bf16[1024,256]{1,0:T(8,128)(2,1)}, u32[]{:S(2)}) copy-start(bf16[1024,256]{1,0:T(8,128)(2,1)} %param.18) | copy-start | bytes 1572868
  21.5 10.5 %copy-start.2 = (bf16[1024,512]{1,0:T(8,128)(2,1)S(1)}, bf16[1024,512]{1,0:T(8,128)(2,1)}, u32[]{:S(2)}) copy-start(bf16[1024,512]{1,0:T(8,128)(2,1)} %param.17) | copy-start | bytes 3145732
  22.8 10.5 %collective-permute-start.2 = (bf16[256,256]{1,0:T(8,128)(2,1)S(1)}, bf16[256,256]{1,0:T(8,128)(2,1)S(1)}, u32[]{:S(2)}, u32[]{:S(2)}) collective-permute-start(bf16[256,256]{1,0:T(8,128)(2,1)S(1)} %get-tuple-element.125), channel_id=1, source_target_pairs={{0,1},{1,0},{2,3},{3,2},{4,5},{5,4},{6,7},{7,6},{8,9},{9,8},{10,11... | collective-permute-start | bytes 393224 | tf_op jit(solution)/shard_map/ppermute | solution.py:35
  26.1 7.2 %collective-permute-start.3 = (bf16[256,256]{1,0:T(8,128)(2,1)S(1)}, bf16[256,256]{1,0:T(8,128)(2,1)S(1)}, u32[]{:S(2)}, u32[]{:S(2)}) collective-permute-start(bf16[256,256]{1,0:T(8,128)(2,1)S(1)} %get-tuple-element.125), channel_id=1, source_target_pairs={{0,2},{2,0},{1,3},{3,1},{4,6},{6,4},{5,7},{7,5},{8,10},{10,8},{9,1... | collective-permute-start | bytes 393224 | tf_op jit(solution)/shard_map/ppermute | solution.py:35
  27.8 7.9 %collective-permute-start.4 = (bf16[256,256]{1,0:T(8,128)(2,1)S(1)}, bf16[256,256]{1,0:T(8,128)(2,1)S(1)}, u32[]{:S(2)}, u32[]{:S(2)}) collective-permute-start(bf16[256,256]{1,0:T(8,128)(2,1)S(1)} %get-tuple-element.125), channel_id=1, source_target_pairs={{0,4},{4,0},{1,5},{5,1},{2,6},{6,2},{3,7},{7,3},{8,12},{12,8},{9,1... | collective-permute-start | bytes 393224 | tf_op jit(solution)/shard_map/ppermute | solution.py:35
  29.4 9.0 %collective-permute-start.5 = (bf16[256,256]{1,0:T(8,128)(2,1)S(1)}, bf16[256,256]{1,0:T(8,128)(2,1)S(1)}, u32[]{:S(2)}, u32[]{:S(2)}) collective-permute-start(bf16[256,256]{1,0:T(8,128)(2,1)S(1)} %get-tuple-element.125), channel_id=1, source_target_pairs={{0,8},{8,0},{1,9},{9,1},{2,10},{10,2},{3,11},{11,3},{4,12},{12,4},... | collective-permute-start | bytes 393224 | tf_op jit(solution)/shard_map/ppermute | solution.py:35
  38.9 23.4 %copy-start.1 = (bf16[512,1024]{1,0:T(8,128)(2,1)S(1)}, bf16[512,1024]{1,0:T(8,128)(2,1)}, u32[]{:S(2)}) copy-start(bf16[512,1024]{1,0:T(8,128)(2,1)} %param.19) | copy-start | bytes 3145732
where the time goes:
time: 64.1 us; the launch traced here: 63.5 us
  matrix products  35.7 us (56%)
  starting transfers between devices  13 us (20%)
  local copies, waits for them, and re-layouts  6.74 us (11%)
  waiting for transfers between devices  5.05 us (8%)
  between operations  2.76 us (4%)
    sub x4, matrix products, one_group(): weights = jnp.where(allowed, jnp.exp(scores - row_max), 0.0)  13.6 us
    dot_general x4, matrix products, one_group(): jnp.einsum('krj,jkd->rkd', shares, value_head_rows, preferred_element_typ...  9.3 us
    ppermute x4, starting transfers between devices, swapped(): return lax.ppermute(block, axis, route)  9.14 us
    sub x1, matrix products, attend_rows(): weights = jnp.where(allowed, jnp.exp(scores - row_max), 0.0)  6.61 us
    ppermute x4, waiting for transfers between devices, swapped(): return lax.ppermute(block, axis, route)  5.05 us
    dot_general x1, matrix products, attend_rows(): jnp.einsum('kgrj,jkd->rkgd', shares, value_head_rows, preferred_element_t...  3.53 us
    ppermute x1, starting transfers between devices, with_halo(): lax.ppermute(tail, axis, [(i, (i + 1) % count) for i in range(ends)])  2.53 us
    unnamed x16, local copies, waits for them, and re-layouts  2.48 us
  transfers between devices with their start and end apart: 6, of which 2 were waited for; matrix products, arithmetic and copies ran while one was open for 9% of the time, Pallas kernels for 0%

commit v1 on v0

v1 whole, which is shorter than its diff:
```python
import functools

import jax
import jax.numpy as jnp
from jax import lax
from jax.experimental import pallas as pl
from jax.experimental.pallas import tpu as pltpu
from jax.sharding import PartitionSpec as P

QUERY_HEADS = 8
HEAD_SIZE = 64
MESH = pl.DeviceIdType.MESH
HIDE = -1e30
NT = (((1,), (1,)), ((), ()))


def dot_nt(a, b):
    return lax.dot_general(a, b, NT, preferred_element_type=jnp.float32)


def dot(a, b):
    return jnp.dot(a, b, preferred_element_type=jnp.float32)


def low_half(shape):
    return lax.broadcasted_iota(jnp.int32, shape, 1) < HEAD_SIZE


def rolled(x):
    return jnp.concatenate([x[:, HEAD_SIZE:], x[:, :HEAD_SIZE]], axis=1)


def spread(keys, values, ones, kx, vx, slot):
    low = low_half(keys.shape)
    none = jnp.zeros_like(keys)
    keys = keys * jnp.bfloat16(HEAD_SIZE ** (-0.5))
    first, second = jnp.where(low, keys, none), jnp.where(low, none, keys)
    kx[slot, 0, 0] = first
    kx[slot, 0, 1] = rolled(first)
    kx[slot, 1, 0] = rolled(second)
    kx[slot, 1, 1] = second
    first, second = jnp.where(low, values, ones), jnp.where(low, ones, values)
    vx[slot, 0, 0] = first
    vx[slot, 0, 1] = rolled(first)
    vx[slot, 1, 0] = rolled(second)
    vx[slot, 1, 1] = second


def row_max(parts):
    top = jnp.max(parts[0], axis=1, keepdims=True)
    for part in parts[1:]:
        top = jnp.maximum(top, jnp.max(part, axis=1, keepdims=True))
    return top


def weight(scores, top):
    return jnp.exp((scores - top).astype(jnp.bfloat16))


def joined(even, odd):
    low = low_half(even.shape)
    return (jnp.where(low, even, odd) / rolled(jnp.where(low, odd, even))).astype(jnp.bfloat16)


def body(
    n,
    levels,
    q_hbm,
    kv_hbm,
    res_hbm,
    extent,
    mask,
    wo1_hbm,
    wq2_hbm,
    wkv2_hbm,
    wo2_hbm,
    out_hbm,
    q,
    kv,
    halo,
    res,
    wo1,
    wq2,
    wkv2,
    wo2,
    kv2,
    kv2_in,
    kx,
    vx,
    tops,
    accs,
    att,
    hid,
    out,
    local_sem,
    send_sem,
    recv_sem,
):
    rows = q.shape[0]
    half = rows // 2
    pairs = q.shape[1] // (2 * HEAD_SIZE)
    per_group = pairs // 2
    me = lax.axis_index("seq")
    loads = [
        pltpu.make_async_copy(src, dst, local_sem.at[i])
        for i, (src, dst) in enumerate(
            (
                (kv_hbm, kv),
                (q_hbm, q),
                (wo1_hbm, wo1),
                (res_hbm, res),
                (wkv2_hbm, wkv2),
                (wq2_hbm, wq2),
                (wo2_hbm, wo2),
            )
        )
    ]
    barrier = pltpu.get_barrier_semaphore()
    has_left, has_right = me > 0, me < n - 1

    @pl.when(has_left)
    def _():
        pl.semaphore_signal(barrier, inc=1, device_id={"seq": me - 1}, device_id_type=MESH)

    @pl.when(has_right)
    def _():
        pl.semaphore_signal(barrier, inc=1, device_id={"seq": me + 1}, device_id_type=MESH)

    def partner(level):
        bit = lax.rem(lax.div(me, 1 << level), 2)
        return me + (1 << level) * (1 - 2 * bit)

    for level in range(levels):
        pl.semaphore_signal(barrier, inc=1, device_id={"seq": partner(level)}, device_id_type=MESH)
    for load in loads:
        load.start()
    ends = has_left.astype(jnp.int32) + has_right.astype(jnp.int32)
    pl.semaphore_wait(barrier, levels + ends)

    def to_right():
        return pltpu.make_async_remote_copy(
            kv_hbm, halo.at[0], send_sem.at[0], recv_sem.at[0],
            device_id={"seq": me + 1}, device_id_type=MESH,
        )

    def to_left():
        return pltpu.make_async_remote_copy(
            kv_hbm, halo.at[1], send_sem.at[1], recv_sem.at[1],
            device_id={"seq": me - 1}, device_id_type=MESH,
        )

    @pl.when(has_right)
    def _():
        to_right().start()

    @pl.when(has_left)
    def _():
        to_left().start()

    wide = 2 * HEAD_SIZE
    ones = jnp.ones((rows, wide), jnp.bfloat16)
    zeros = jnp.zeros((rows, wide), jnp.bfloat16)

    loads[0].wait()
    spread(kv[:, :wide], kv[:, wide:], ones, kx, vx, 0)
    loads[1].wait()
    row = lax.broadcasted_iota(jnp.int32, (rows, rows), 0)
    col = lax.broadcasted_iota(jnp.int32, (rows, rows), 1)
    apart = jnp.abs(row - col)
    for pair in range(pairs):
        queries = q[:, pair * wide : (pair + 1) * wide]
        for odd in range(2):
            h = 2 * pair + odd
            scores = dot_nt(queries, kx[0, pair // per_group, odd])
            scores = jnp.where(apart <= extent[h], scores, HIDE)
            top = row_max([scores])
            tops[h] = jnp.broadcast_to(top, (rows, wide))
            accs[h] = dot(weight(scores, top), vx[0, pair // per_group, odd])

    @pl.when(has_left)
    def _():
        to_right().wait_recv()

    @pl.when(jnp.logical_not(has_left))
    def _():
        halo[0] = jnp.zeros(halo.shape[1:], jnp.bfloat16)

    @pl.when(has_right)
    def _():
        to_left().wait_recv()

    @pl.when(jnp.logical_not(has_right))
    def _():
        halo[1] = jnp.zeros(halo.shape[1:], jnp.bfloat16)

    for side in range(2):
        spread(halo[side, :, :wide], halo[side, :, wide:], ones, kx, vx, 1 + side)
    far = 4 * n * rows
    left_off = rows + jnp.where(has_left, 0, far)
    right_off = rows + jnp.where(has_right, 0, far)
    for tile in range(2):
        here = slice(tile * half, (tile + 1) * half)
        left = slice(0, rows) if tile == 0 else slice(half, rows)
        right = slice(0, half) if tile == 0 else slice(0, rows)
        left_apart = (row - col)[here, left] + left_off
        right_apart = (col - row)[here, right] + right_off
        for pair in range(pairs):
            queries = q[here, pair * wide : (pair + 1) * wide]
            group = pair // per_group
            done = []
            for odd in range(2):
                h = 2 * pair + odd
                a = dot_nt(queries, kx[1, group, odd, left])
                b = dot_nt(queries, kx[2, group, odd, right])
                a = jnp.where(left_apart <= extent[h], a, HIDE)
                b = jnp.where(right_apart <= extent[h], b, HIDE)
                before = tops[h, here, 0:1]
                top = jnp.maximum(before, row_max([a, b]))
                acc = accs[h, here] * jnp.exp(before - top)
                acc += dot(weight(a, top), vx[1, group, odd, left])
                acc += dot(weight(b, top), vx[2, group, odd, right])
                done.append(acc)
            att[here, pair * wide : (pair + 1) * wide] = joined(*done)

    loads[2].wait()
    loads[3].wait()
    hidden = (dot(att[...], wo1[...]) + res[...].astype(jnp.float32)).astype(jnp.bfloat16)
    hid[...] = hidden
    values = hidden.astype(jnp.float32)
    scale = lax.rsqrt(jnp.mean(values * values, axis=-1, keepdims=True) + 1e-05)
    normed = (values * scale).astype(jnp.bfloat16)
    loads[4].wait()
    kv2[...] = dot(normed, wkv2[...]).astype(jnp.bfloat16)
    swaps = [
        pltpu.make_async_remote_copy(
            kv2, kv2_in.at[level], send_sem.at[2 + level], recv_sem.at[2 + level],
            device_id={"seq": partner(level)}, device_id_type=MESH,
        )
        for level in range(levels)
    ]
    for swap in reversed(swaps):
        swap.start()
    loads[5].wait()
    q[...] = dot(normed, wq2[...]).astype(jnp.bfloat16)
    own = kv2[...]
    spread(own[:, :wide], own[:, wide:], ones, kx, vx, 0)

    chunks = [list(range(0, min(3, levels + 1)))]
    while chunks[-1][-1] < levels:
        first = chunks[-1][-1] + 1
        chunks.append(list(range(first, min(first + 2, levels + 1))))
    for chunk in chunks:
        for slot in chunk:
            if slot > 0:
                swaps[slot - 1].wait_recv()
                seen = mask[0, slot - 1] == 1
                spread(
                    jnp.where(seen, kv2_in[slot - 1, :, :wide], kv2[:, :wide]),
                    jnp.where(seen, kv2_in[slot - 1, :, wide:], zeros),
                    jnp.where(seen, ones, zeros),
                    kx, vx, slot,
                )
        for pair in range(pairs):
            queries = q[:, pair * wide : (pair + 1) * wide]
            group = pair // per_group
            done = []
            for odd in range(2):
                h = 2 * pair + odd
                parts = [dot_nt(queries, kx[slot, group, odd]) for slot in chunk]
                top = row_max(parts)
                acc = None
                if chunk[0] > 0:
                    before = tops[h, :, 0:1]
                    top = jnp.maximum(before, top)
                    acc = accs[h] * jnp.exp(before - top)
                for slot, part in zip(chunk, parts):
                    term = dot(weight(part, top), vx[slot, group, odd])
                    acc = term if acc is None else acc + term
                if chunk[-1] < levels:
                    tops[h] = jnp.broadcast_to(top, (rows, wide))
                    accs[h] = acc
                done.append(acc)
            if chunk[-1] == levels:
                att[:, pair * wide : (pair + 1) * wide] = joined(*done)

    loads[6].wait()
    stores = []
    for tile in range(2):
        here = slice(tile * half, (tile + 1) * half)
        out[here] = (dot(att[here], wo2[...]) + hid[here].astype(jnp.float32)).astype(jnp.bfloat16)
        stores.append(
            pltpu.make_async_copy(
                out.at[pl.ds(tile * half, half)],
                out_hbm.at[pl.ds(tile * half, half)],
                local_sem.at[7 + tile],
            )
        )
        stores[-1].start()
    for swap in swaps:
        swap.wait_send()

    @pl.when(has_right)
    def _():
        to_right().wait_send()

    @pl.when(has_left)
    def _():
        to_left().wait_send()

    for store in stores:
        store.wait()


def shards(
    n, residual, layer_queries, layer_keyvals, head_window_extent, block_mask,
    first_out, second_query, second_keyval, second_out,
):
    levels = n.bit_length() - 1
    rows, width = residual.shape
    query_width = layer_queries.shape[1]
    kv_width = layer_keyvals.shape[1]
    wide = 2 * HEAD_SIZE
    blocks = max(3, levels + 1)
    bf16, f32 = jnp.bfloat16, jnp.float32
    anywhere = pl.BlockSpec(memory_space=pl.ANY)
    scalars = pl.BlockSpec(memory_space=pltpu.SMEM)
    return pl.pallas_call(
        functools.partial(body, n, levels),
        name="two_layers",
        out_shape=jax.ShapeDtypeStruct((rows, width), bf16),
        in_specs=[anywhere] * 3 + [scalars] * 2 + [anywhere] * 4,
        out_specs=anywhere,
        scratch_shapes=[
            pltpu.VMEM((rows, query_width), bf16),
            pltpu.VMEM((rows, kv_width), bf16),
            pltpu.VMEM((2, rows, kv_width), bf16),
            pltpu.VMEM((rows, width), bf16),
            pltpu.VMEM(first_out.shape, bf16),
            pltpu.VMEM(second_query.shape, bf16),
            pltpu.VMEM(second_keyval.shape, bf16),
            pltpu.VMEM(second_out.shape, bf16),
            pltpu.VMEM((rows, kv_width), bf16),
            pltpu.VMEM((levels, rows, kv_width), bf16),
            pltpu.VMEM((blocks, 2, 2, rows, wide), bf16),
            pltpu.VMEM((blocks, 2, 2, rows, wide), bf16),
            pltpu.VMEM((QUERY_HEADS, rows, wide), f32),
            pltpu.VMEM((QUERY_HEADS, rows, wide), f32),
            pltpu.VMEM((rows, query_width), bf16),
            pltpu.VMEM((rows, width), bf16),
            pltpu.VMEM((rows, width), bf16),
            pltpu.SemaphoreType.DMA((9,)),
            pltpu.SemaphoreType.DMA((2 + levels,)),
            pltpu.SemaphoreType.DMA((2 + levels,)),
        ],
        compiler_params=pltpu.CompilerParams(collective_id=0, has_side_effects=True),
    )(
        layer_queries, layer_keyvals, residual, head_window_extent, block_mask,
        first_out, second_query, second_keyval, second_out,
    )


def solution(mesh):
    placed = (
        P(("groups", "seq"), None),
        P(("groups", "seq"), None),
        P(("groups", "seq"), None),
        P(),
        P("seq", None),
        P(),
        P(),
        P(),
        P(),
    )
    return jax.shard_map(
        functools.partial(shards, mesh.shape["seq"]),
        mesh=mesh, in_specs=placed, out_specs=P(("groups", "seq"), None), check_vma=False,
    )
```

time: 64.1 us -> 31.4 us (0.49)
  matrix products: 35.7 us -> 0 us
  Pallas kernels: 0 us -> 29.4 us
  starting transfers between devices: 13 us -> 0 us
  waiting for transfers between devices: 5.05 us -> 0 us
  local copies, waits for them, and re-layouts: 6.74 us -> 1.87 us
  between operations: 2.76 us -> 0.01 us
    pallas_call x0 -> x1, Pallas kernels: none -> 29.4 us  [shards(): pl.pallas_call(functools.partial(body, n, levels), name='two_layers', out...]
    sub x5 -> x0, matrix products: 20.2 us -> none  [the longest x4 13.6 us: one_group(): weights = jnp.where(allowed, jnp.exp(scores - row_max), 0.0)]
    dot_general x9 -> x0, matrix products: 15.5 us -> none  [the longest x4 9.3 us: one_group(): jnp.einsum('krj,jkd->rkd', shares, value_head_rows, preferred_element_typ...]
    ppermute x6 -> x0, starting transfers between devices: 13 us -> none  [the longest x4 9.14 us: swapped(): return lax.ppermute(block, axis, route)]
    ppermute x6 -> x0, waiting for transfers between devices: 5.05 us -> none  [the longest x4 5.05 us: swapped(): return lax.ppermute(block, axis, route)]
    slice x7 -> x0, local copies, waits for them, and re-layouts: 2.21 us -> none  [the longest x1 1.47 us: shards(): key_flags.append(block_mask[0, level] == 1)]
    convert_element_type x1 -> x0, local copies, waits for them, and re-layouts: 0.84 us -> none  [shards(): jnp.dot(normed, second_query, preferred_element_type=jnp.float32)]
    le x1 -> x0, local copies, waits for them, and re-layouts: 0.74 us -> none  [window_block(): distance[None, None] <= window_extent]
  transfers between devices with their start and end apart: 6 -> 0, of which waited for: 2 -> 0; matrix products, arithmetic and copies ran while one was open for 9% -> 0% of each run, Pallas kernels for 0% -> 0%
where the time goes in v1:
time: 31.4 us; the launch traced here: 31.3 us
  Pallas kernels  29.4 us (94%)
  local copies, waits for them, and re-layouts  1.87 us (6%)
    pallas_call x1, Pallas kernels, shards(): pl.pallas_call(functools.partial(body, n, levels), name='two_layers', out...  29.4 us
    unnamed x1, local copies, waits for them, and re-layouts  1.87 us

profile of v1, /device:TPU:0, one launch (start us, length us, event | category | flops | bytes accessed | tf_op | source)
XLA Modules:
  0.0 31.3 jit_solution(11450029151712998019)
XLA Ops:
  0.0 29.4 %two_layers.1 = bf16[256,1024]{1,0:T(8,128)(2,1)} custom-call(bf16[256,512]{1,0:T(8,128)(2,1)} %q_hbm.1, bf16[256,256]{1,0:T(8,128)(2,1)} %kv_hbm.1, bf16[256,1024]{1,0:T(8,128)(2,1)} %res_hbm.1, s32[8]{0:T(128)} %extent.1, s32[1,4]{1,0:T(1,128)} %mask.1, bf16[512,1024]{1,0:T(8,128)(2,1)} %wo1_hbm.1, bf16[1024,512]{1,0:T(8,128)(2,1)} %wq2_hbm.1, ...), custom_call_target="tpu_custom_call" | custom-call | tf_op jit(solution)/shard_map/two_layers/pallas_call | solution.py:327
  29.4 1.9 %copy.11 = bf16[256,1024]{1,0:T(8,128)(2,1)} copy(bf16[256,1024]{1,0:T(8,128)(2,1)} %two_layers.1) | data formatting | bytes 1048576

commit v2 on v1

v2 whole, which is shorter than its diff:
```python
import functools

import jax
import jax.numpy as jnp
from jax import lax
from jax.experimental import pallas as pl
from jax.experimental.pallas import tpu as pltpu
from jax.sharding import PartitionSpec as P

QUERY_HEADS = 8
HEAD_SIZE = 64
MESH = pl.DeviceIdType.MESH
HIDE = -1e30
TOTALS = 16
NT = (((1,), (1,)), ((), ()))


def dot_nt(a, b):
    return lax.dot_general(a, b, NT, preferred_element_type=jnp.float32)


def dot(a, b):
    return jnp.dot(a, b, preferred_element_type=jnp.float32)


def rolled(x):
    return jnp.concatenate([x[:, HEAD_SIZE:], x[:, :HEAD_SIZE]], axis=1)


def spread(keys, values, ones, kx, vt, slot):
    low = lax.broadcasted_iota(jnp.int32, keys.shape, 1) < HEAD_SIZE
    none = jnp.zeros_like(keys)
    first, second = jnp.where(low, keys, none), jnp.where(low, none, keys)
    kx[slot, 0, 0] = first
    kx[slot, 0, 1] = rolled(first)
    kx[slot, 1, 0] = rolled(second)
    kx[slot, 1, 1] = second
    for group in range(2):
        vt[slot, group, :HEAD_SIZE] = values[group * HEAD_SIZE : (group + 1) * HEAD_SIZE]
        vt[slot, group, HEAD_SIZE:] = ones


def col_max(parts):
    top = jnp.max(parts[0], axis=0, keepdims=True)
    for part in parts[1:]:
        top = jnp.maximum(top, jnp.max(part, axis=0, keepdims=True))
    return top


def weight(scores, top):
    return jnp.exp((scores - top).astype(jnp.bfloat16))


def shared(acc):
    return acc[:HEAD_SIZE] * (1.0 / acc[HEAD_SIZE : HEAD_SIZE + 1])


def body(
    n, levels,
    q_hbm, kv_hbm, res_hbm, extent, mask, wo1_hbm, wq2_hbm, wkv2_hbm,
    att_out, hid_out,
    q, kv, halo, res, wo1, wq2, wkv2, kv2, kv2_in, kx, vt, tops, accs, att, hid,
    local_sem, send_sem, recv_sem,
):
    rows = q.shape[0]
    wide = 2 * HEAD_SIZE
    pairs = q.shape[1] // wide
    per_group = pairs // 2
    scaled = jnp.bfloat16(HEAD_SIZE ** (-0.5))
    me = lax.axis_index("seq")
    loads = [
        pltpu.make_async_copy(src, dst, local_sem.at[i])
        for i, (src, dst) in enumerate(
            (
                (kv_hbm, kv),
                (q_hbm, q),
                (wo1_hbm, wo1),
                (res_hbm, res),
                (wkv2_hbm, wkv2),
                (wq2_hbm, wq2),
            )
        )
    ]
    barrier = pltpu.get_barrier_semaphore()
    has_left, has_right = me > 0, me < n - 1

    @pl.when(has_left)
    def _():
        pl.semaphore_signal(barrier, inc=1, device_id={"seq": me - 1}, device_id_type=MESH)

    @pl.when(has_right)
    def _():
        pl.semaphore_signal(barrier, inc=1, device_id={"seq": me + 1}, device_id_type=MESH)

    def partner(level):
        bit = lax.rem(lax.div(me, 1 << level), 2)
        return me + (1 << level) * (1 - 2 * bit)

    for level in range(levels):
        pl.semaphore_signal(barrier, inc=1, device_id={"seq": partner(level)}, device_id_type=MESH)
    for load in loads:
        load.start()
    ends = has_left.astype(jnp.int32) + has_right.astype(jnp.int32)
    pl.semaphore_wait(barrier, levels + ends)

    def to_right():
        return pltpu.make_async_remote_copy(
            kv_hbm, halo.at[0], send_sem.at[0], recv_sem.at[0],
            device_id={"seq": me + 1}, device_id_type=MESH,
        )

    def to_left():
        return pltpu.make_async_remote_copy(
            kv_hbm, halo.at[1], send_sem.at[1], recv_sem.at[1],
            device_id={"seq": me - 1}, device_id_type=MESH,
        )

    @pl.when(has_right)
    def _():
        to_right().start()

    @pl.when(has_left)
    def _():
        to_left().start()

    ones = jnp.ones((TOTALS, rows), jnp.bfloat16)

    loads[0].wait()
    spread(kv[:, :wide] * scaled, kv[:, wide:].T, ones, kx, vt, 0)
    loads[1].wait()
    key = lax.broadcasted_iota(jnp.int32, (rows, rows), 0)
    query = lax.broadcasted_iota(jnp.int32, (rows, rows), 1)
    apart = jnp.abs(key - query)
    for pair in range(pairs):
        queries = q[:, pair * wide : (pair + 1) * wide]
        for odd in range(2):
            h = 2 * pair + odd
            scores = dot_nt(kx[0, pair // per_group, odd], queries)
            scores = jnp.where(apart <= extent[h], scores, HIDE)
            top = col_max([scores])
            tops[h] = jnp.broadcast_to(top, tops.shape[1:])
            accs[h] = dot(vt[0, pair // per_group], weight(scores, top))

    @pl.when(has_left)
    def _():
        to_right().wait_recv()

    @pl.when(jnp.logical_not(has_left))
    def _():
        halo[0] = jnp.zeros(halo.shape[1:], jnp.bfloat16)

    @pl.when(has_right)
    def _():
        to_left().wait_recv()

    @pl.when(jnp.logical_not(has_right))
    def _():
        halo[1] = jnp.zeros(halo.shape[1:], jnp.bfloat16)

    for side in range(2):
        spread(halo[side, :, :wide] * scaled, halo[side, :, wide:].T, ones, kx, vt, 1 + side)
    far = 4 * n * rows
    left_apart = query - key + rows + jnp.where(has_left, 0, far)
    right_apart = key - query + rows + jnp.where(has_right, 0, far)
    for pair in range(pairs):
        queries = q[:, pair * wide : (pair + 1) * wide]
        group = pair // per_group
        done = []
        for odd in range(2):
            h = 2 * pair + odd
            a = dot_nt(kx[1, group, odd], queries)
            b = dot_nt(kx[2, group, odd], queries)
            a = jnp.where(left_apart <= extent[h], a, HIDE)
            b = jnp.where(right_apart <= extent[h], b, HIDE)
            before = tops[h, 0:1]
            top = jnp.maximum(before, col_max([a, b]))
            acc = accs[h] * jnp.exp(before - top)
            acc += dot(vt[1, group], weight(a, top))
            acc += dot(vt[2, group], weight(b, top))
            done.append(shared(acc))
        att[:, pair * wide : (pair + 1) * wide] = jnp.concatenate(done, axis=0).astype(jnp.bfloat16).T

    loads[2].wait()
    loads[3].wait()
    hidden = (dot(att[...], wo1[...]) + res[...].astype(jnp.float32)).astype(jnp.bfloat16)
    hid[...] = hidden
    values = hidden.astype(jnp.float32)
    scale = lax.rsqrt(jnp.mean(values * values, axis=-1, keepdims=True) + 1e-05)
    normed = (values * scale).astype(jnp.bfloat16)
    loads[4].wait()
    keyvals = dot(normed, wkv2[...]).astype(jnp.bfloat16)
    kv2[:rows] = keyvals[:, :wide] * scaled
    turned = keyvals[:, wide:].T
    for part in range(rows // wide):
        kv2[rows + part * wide : rows + (part + 1) * wide] = turned[:, part * wide : (part + 1) * wide]
    swaps = [
        pltpu.make_async_remote_copy(
            kv2, kv2_in.at[level], send_sem.at[2 + level], recv_sem.at[2 + level],
            device_id={"seq": partner(level)}, device_id_type=MESH,
        )
        for level in range(levels)
    ]
    for swap in reversed(swaps):
        swap.start()
    keep_hidden = pltpu.make_async_copy(hid, hid_out, local_sem.at[6])
    keep_hidden.start()
    loads[5].wait()
    q[...] = dot(normed, wq2[...]).astype(jnp.bfloat16)
    spread(kv2[:rows], turned, ones, kx, vt, 0)

    chunks = [list(range(0, min(3, levels + 1)))]
    while chunks[-1][-1] < levels:
        first = chunks[-1][-1] + 1
        chunks.append(list(range(first, min(first + 2, levels + 1))))
    for chunk in chunks:
        for slot in chunk:
            if slot > 0:
                swaps[slot - 1].wait_recv()
                seen = mask[0, slot - 1] == 1
                came = jnp.concatenate(
                    [
                        kv2_in[slot - 1, rows + part * wide : rows + (part + 1) * wide]
                        for part in range(rows // wide)
                    ],
                    axis=1,
                )
                spread(
                    jnp.where(seen, kv2_in[slot - 1, :rows], kv2[:rows]),
                    jnp.where(seen, came, jnp.zeros_like(came)),
                    jnp.where(seen, ones, jnp.zeros_like(ones)),
                    kx, vt, slot,
                )
        for pair in range(pairs):
            queries = q[:, pair * wide : (pair + 1) * wide]
            group = pair // per_group
            done = []
            for odd in range(2):
                h = 2 * pair + odd
                parts = [dot_nt(kx[slot, group, odd], queries) for slot in chunk]
                top = col_max(parts)
                acc = None
                if chunk[0] > 0:
                    before = tops[h, 0:1]
                    top = jnp.maximum(before, top)
                    acc = accs[h] * jnp.exp(before - top)
                for slot, part in zip(chunk, parts):
                    term = dot(vt[slot, group], weight(part, top))
                    acc = term if acc is None else acc + term
                if chunk[-1] < levels:
                    tops[h] = jnp.broadcast_to(top, tops.shape[1:])
                    accs[h] = acc
                else:
                    done.append(shared(acc))
            if done:
                att[:, pair * wide : (pair + 1) * wide] = (
                    jnp.concatenate(done, axis=0).astype(jnp.bfloat16).T
                )

    keep_att = pltpu.make_async_copy(att, att_out, local_sem.at[7])
    keep_att.start()
    for swap in swaps:
        swap.wait_send()

    @pl.when(has_right)
    def _():
        to_right().wait_send()

    @pl.when(has_left)
    def _():
        to_left().wait_send()

    keep_hidden.wait()
    keep_att.wait()


def shards(
    n, residual, layer_queries, layer_keyvals, head_window_extent, block_mask,
    first_out, second_query, second_keyval, second_out,
):
    levels = n.bit_length() - 1
    rows, width = residual.shape
    query_width = layer_queries.shape[1]
    kv_width = layer_keyvals.shape[1]
    wide = 2 * HEAD_SIZE
    blocks = max(3, levels + 1)
    bf16, f32 = jnp.bfloat16, jnp.float32
    anywhere = pl.BlockSpec(memory_space=pl.ANY)
    stays = pl.BlockSpec(memory_space=pltpu.HBM)
    scalars = pl.BlockSpec(memory_space=pltpu.SMEM)
    att, hidden = pl.pallas_call(
        functools.partial(body, n, levels),
        name="two_layers",
        out_shape=(
            jax.ShapeDtypeStruct((rows, query_width), bf16),
            jax.ShapeDtypeStruct((rows, width), bf16),
        ),
        in_specs=[stays] * 3 + [scalars] * 2 + [stays] * 3,
        out_specs=(anywhere, anywhere),
        scratch_shapes=[
            pltpu.VMEM((rows, query_width), bf16),
            pltpu.VMEM((rows, kv_width), bf16),
            pltpu.VMEM((2, rows, kv_width), bf16),
            pltpu.VMEM((rows, width), bf16),
            pltpu.VMEM(first_out.shape, bf16),
            pltpu.VMEM(second_query.shape, bf16),
            pltpu.VMEM(second_keyval.shape, bf16),
            pltpu.VMEM((2 * rows, wide), bf16),
            pltpu.VMEM((levels, 2 * rows, wide), bf16),
            pltpu.VMEM((blocks, 2, 2, rows, wide), bf16),
            pltpu.VMEM((blocks, 2, HEAD_SIZE + TOTALS, rows), bf16),
            pltpu.VMEM((QUERY_HEADS, 8, rows), f32),
            pltpu.VMEM((QUERY_HEADS, HEAD_SIZE + TOTALS, rows), f32),
            pltpu.VMEM((rows, query_width), bf16),
            pltpu.VMEM((rows, width), bf16),
            pltpu.SemaphoreType.DMA((8,)),
            pltpu.SemaphoreType.DMA((2 + levels,)),
            pltpu.SemaphoreType.DMA((2 + levels,)),
        ],
        compiler_params=pltpu.CompilerParams(
            collective_id=0, has_side_effects=True
        ),
    )(
        layer_queries, layer_keyvals, residual, head_window_extent, block_mask,
        first_out, second_query, second_keyval,
    )
    output = jnp.dot(att, second_out, preferred_element_type=f32) + hidden.astype(f32)
    return output.astype(bf16)


def solution(mesh):
    placed = (
        P(("groups", "seq"), None),
        P(("groups", "seq"), None),
        P(("groups", "seq"), None),
        P(),
        P("seq", None),
        P(),
        P(),
        P(),
        P(),
    )
    return jax.shard_map(
        functools.partial(shards, mesh.shape["seq"]),
        mesh=mesh, in_specs=placed, out_specs=P(("groups", "seq"), None), check_vma=False,
    )
```

time: 31.4 us -> 28.1 us (0.89)
  Pallas kernels: 29.4 us -> 25.6 us
  matrix products: 0 us -> 2.36 us
  local copies, waits for them, and re-layouts: 1.87 us -> 0.01 us
    pallas_call x1, Pallas kernels: 29.4 us -> 25.6 us  [shards(): pl.pallas_call(functools.partial(body, n, levels), name='two_layers', out...]
    dot_general x0 -> x1, matrix products: none -> 2.36 us  [shards(): jnp.dot(att, second_out, preferred_element_type=f32) + hidden.astype(f32)]
    unnamed x1 -> x2, local copies, waits for them, and re-layouts: 1.87 us -> 0.01 us
where the time goes in v2:
time: 28.1 us; the launch traced here: 28 us
  Pallas kernels  25.6 us (91%)
  matrix products  2.36 us (8%)
    pallas_call x1, Pallas kernels, shards(): pl.pallas_call(functools.partial(body, n, levels), name='two_layers', out...  25.6 us
    dot_general x1, matrix products, shards(): jnp.dot(att, second_out, preferred_element_type=f32) + hidden.astype(f32)  2.36 us

profile of v2, /device:TPU:0, one launch (start us, length us, event | category | flops | bytes accessed | tf_op | source)
XLA Modules:
  0.0 28.0 jit_solution(12317367152900662939)
XLA Ops:
  0.0 0.0 copy-start
  0.0 25.6 %two_layers.1 = (bf16[256,512]{1,0:T(8,128)(2,1)}, bf16[256,1024]{1,0:T(8,128)(2,1)}) custom-call(bf16[256,512]{1,0:T(8,128)(2,1)} %q_hbm.1, bf16[256,256]{1,0:T(8,128)(2,1)} %kv_hbm.1, bf16[256,1024]{1,0:T(8,128)(2,1)} %res_hbm.1, s32[8]{0:T(128)} %extent.1, s32[1,4]{1,0:T(1,128)} %mask.1, bf16[512,1024]{1,0:T(8,128)(2,1)} %wo1_hbm.1, ...), custom_call_target="tpu_custom_call" | custom-call | tf_op jit(solution)/shard_map/two_layers/pallas_call | solution.py:290
  25.6 0.0 copy-done
  25.6 2.4 %fusion = bf16[256,1024]{1,0:T(8,128)(2,1)} fusion(bf16[256,512]{1,0:T(8,128)(2,1)} %get-tuple-element.7, bf16[512,1024]{1,0:T(8,128)(2,1)S(1)} %copy-done, bf16[256,1024]{1,0:T(8,128)(2,1)} %get-tuple-element.8), kind=kOutput, calls=%fused_computation.1 | convolution fusion | flops 269221888 | bytes 2359296 | tf_op jit(solution)/shard_map/dot_general | solution.py:326
Async XLA Ops:
  0.0 25.6 %copy-start = (bf16[512,1024]{1,0:T(8,128)(2,1)S(1)}, bf16[512,1024]{1,0:T(8,128)(2,1)}, u32[]{:S(2)}) copy-start(bf16[512,1024]{1,0:T(8,128)(2,1)} %param.17) | copy-start | bytes 3145732

commit v3 on v2

--- a/solution.py
+++ b/solution.py
@@ -49,6 +49,18 @@
 
 def weight(scores, top):
     return jnp.exp((scores - top).astype(jnp.bfloat16))
+
+
+def staggered(steps, scores, weigh, finish):
+    ready, weighed = {}, {}
+    count = len(steps)
+    for at in range(count + 2):
+        if at < count:
+            ready[at] = scores(steps[at])
+        if 0 <= at - 1 < count:
+            weighed[at - 1] = weigh(steps[at - 1], ready.pop(at - 1))
+        if 0 <= at - 2 < count:
+            finish(steps[at - 2], *weighed.pop(at - 2))
 
 
 def shared(acc):
@@ -131,15 +143,32 @@
     key = lax.broadcasted_iota(jnp.int32, (rows, rows), 0)
     query = lax.broadcasted_iota(jnp.int32, (rows, rows), 1)
     apart = jnp.abs(key - query)
-    for pair in range(pairs):
-        queries = q[:, pair * wide : (pair + 1) * wide]
-        for odd in range(2):
-            h = 2 * pair + odd
-            scores = dot_nt(kx[0, pair // per_group, odd], queries)
-            scores = jnp.where(apart <= extent[h], scores, HIDE)
-            top = col_max([scores])
-            tops[h] = jnp.broadcast_to(top, tops.shape[1:])
-            accs[h] = dot(vt[0, pair // per_group], weight(scores, top))
+    heads = list(range(2 * pairs))
+
+    def queries_of(h):
+        pair = h // 2
+        return q[:, pair * wide : (pair + 1) * wide]
+
+    def put(h, share, halves):
+        halves.append(share)
+        if h % 2:
+            both = jnp.concatenate(halves, axis=0).astype(jnp.bfloat16)
+            att[:, h // 2 * wide : (h // 2 + 1) * wide] = both.T
+            halves.clear()
+
+    def own_scores(h):
+        return dot_nt(kx[0, h // 2 // per_group, h % 2], queries_of(h))
+
+    def own_weigh(h, scores):
+        scores = jnp.where(apart <= extent[h], scores, HIDE)
+        top = col_max([scores])
+        tops[h] = jnp.broadcast_to(top, tops.shape[1:])
+        return (weight(scores, top),)
+
+    def own_finish(h, shares):
+        accs[h] = dot(vt[0, h // 2 // per_group], shares)
+
+    staggered(heads, own_scores, own_weigh, own_finish)
 
     @pl.when(has_left)
     def _():
@@ -162,23 +191,25 @@
     far = 4 * n * rows
     left_apart = query - key + rows + jnp.where(has_left, 0, far)
     right_apart = key - query + rows + jnp.where(has_right, 0, far)
-    for pair in range(pairs):
-        queries = q[:, pair * wide : (pair + 1) * wide]
-        group = pair // per_group
-        done = []
-        for odd in range(2):
-            h = 2 * pair + odd
-            a = dot_nt(kx[1, group, odd], queries)
-            b = dot_nt(kx[2, group, odd], queries)
-            a = jnp.where(left_apart <= extent[h], a, HIDE)
-            b = jnp.where(right_apart <= extent[h], b, HIDE)
-            before = tops[h, 0:1]
-            top = jnp.maximum(before, col_max([a, b]))
-            acc = accs[h] * jnp.exp(before - top)
-            acc += dot(vt[1, group], weight(a, top))
-            acc += dot(vt[2, group], weight(b, top))
-            done.append(shared(acc))
-        att[:, pair * wide : (pair + 1) * wide] = jnp.concatenate(done, axis=0).astype(jnp.bfloat16).T
+    halves = []
+
+    def side_scores(h):
+        return [dot_nt(kx[side, h // 2 // per_group, h % 2], queries_of(h)) for side in (1, 2)]
+
+    def side_weigh(h, parts):
+        a = jnp.where(left_apart <= extent[h], parts[0], HIDE)
+        b = jnp.where(right_apart <= extent[h], parts[1], HIDE)
+        before = tops[h, 0:1]
+        top = jnp.maximum(before, col_max([a, b]))
+        return jnp.exp(before - top), weight(a, top), weight(b, top)
+
+    def side_finish(h, fade, a, b):
+        acc = accs[h] * fade
+        acc += dot(vt[1, h // 2 // per_group], a)
+        acc += dot(vt[2, h // 2 // per_group], b)
+        put(h, shared(acc), halves)
+
+    staggered(heads, side_scores, side_weigh, side_finish)
 
     loads[2].wait()
     loads[3].wait()
@@ -230,31 +261,32 @@
                     jnp.where(seen, ones, jnp.zeros_like(ones)),
                     kx, vt, slot,
                 )
-        for pair in range(pairs):
-            queries = q[:, pair * wide : (pair + 1) * wide]
-            group = pair // per_group
-            done = []
-            for odd in range(2):
-                h = 2 * pair + odd
-                parts = [dot_nt(kx[slot, group, odd], queries) for slot in chunk]
-                top = col_max(parts)
-                acc = None
-                if chunk[0] > 0:
-                    before = tops[h, 0:1]
-                    top = jnp.maximum(before, top)
-                    acc = accs[h] * jnp.exp(before - top)
-                for slot, part in zip(chunk, parts):
-                    term = dot(vt[slot, group], weight(part, top))
-                    acc = term if acc is None else acc + term
-                if chunk[-1] < levels:
-                    tops[h] = jnp.broadcast_to(top, tops.shape[1:])
-                    accs[h] = acc
-                else:
-                    done.append(shared(acc))
-            if done:
-                att[:, pair * wide : (pair + 1) * wide] = (
-                    jnp.concatenate(done, axis=0).astype(jnp.bfloat16).T
-                )
+
+        def far_scores(h):
+            return [dot_nt(kx[slot, h // 2 // per_group, h % 2], queries_of(h)) for slot in chunk]
+
+        def far_weigh(h, parts):
+            top = col_max(parts)
+            fade = None
+            if chunk[0] > 0:
+                before = tops[h, 0:1]
+                top = jnp.maximum(before, top)
+                fade = jnp.exp(before - top)
+            if chunk[-1] < levels:
+                tops[h] = jnp.broadcast_to(top, tops.shape[1:])
+            return fade, [weight(part, top) for part in parts]
+
+        def far_finish(h, fade, parts):
+            acc = None if fade is None else accs[h] * fade
+            for slot, part in zip(chunk, parts):
+                term = dot(vt[slot, h // 2 // per_group], part)
+                acc = term if acc is None else acc + term
+            if chunk[-1] < levels:
+                accs[h] = acc
+            else:
+                put(h, shared(acc), halves)
+
+        staggered(heads, far_scores, far_weigh, far_finish)
 
     keep_att = pltpu.make_async_copy(att, att_out, local_sem.at[7])
     keep_att.start()

time: 28.1 us -> 25.7 us (0.915)
  Pallas kernels: 25.6 us -> 23.1 us
    pallas_call x1, Pallas kernels: 25.6 us -> 23.1 us  [shards(): pl.pallas_call(functools.partial(body, n, levels), name='two_layers', out...]
where the time goes in v3:
time: 25.7 us; the launch traced here: 25.5 us
  Pallas kernels  23.1 us (90%)
  matrix products  2.36 us (9%)
    pallas_call x1, Pallas kernels, shards(): pl.pallas_call(functools.partial(body, n, levels), name='two_layers', out...  23.1 us
    dot_general x1, matrix products, shards(): jnp.dot(att, second_out, preferred_element_type=f32) + hidden.astype(f32)  2.36 us

profile of v3, /device:TPU:0, one launch (start us, length us, event | category | flops | bytes accessed | tf_op | source)
XLA Modules:
  0.0 25.5 jit_solution(16119585463527910994)
XLA Ops:
  0.0 0.0 copy-start
  0.0 23.1 %two_layers.1 = (bf16[256,512]{1,0:T(8,128)(2,1)}, bf16[256,1024]{1,0:T(8,128)(2,1)}) custom-call(bf16[256,512]{1,0:T(8,128)(2,1)} %q_hbm.1, bf16[256,256]{1,0:T(8,128)(2,1)} %kv_hbm.1, bf16[256,1024]{1,0:T(8,128)(2,1)} %res_hbm.1, s32[8]{0:T(128)} %extent.1, s32[1,4]{1,0:T(1,128)} %mask.1, bf16[512,1024]{1,0:T(8,128)(2,1)} %wo1_hbm.1, ...), custom_call_target="tpu_custom_call" | custom-call | tf_op jit(solution)/shard_map/two_layers/pallas_call | solution.py:322
  23.1 0.0 copy-done
  23.2 2.4 %fusion = bf16[256,1024]{1,0:T(8,128)(2,1)} fusion(bf16[256,512]{1,0:T(8,128)(2,1)} %get-tuple-element.7, bf16[512,1024]{1,0:T(8,128)(2,1)S(1)} %copy-done, bf16[256,1024]{1,0:T(8,128)(2,1)} %get-tuple-element.8), kind=kOutput, calls=%fused_computation.1 | convolution fusion | flops 269221888 | bytes 2359296 | tf_op jit(solution)/shard_map/dot_general | solution.py:358
Async XLA Ops:
  0.0 23.1 %copy-start = (bf16[512,1024]{1,0:T(8,128)(2,1)S(1)}, bf16[512,1024]{1,0:T(8,128)(2,1)}, u32[]{:S(2)}) copy-start(bf16[512,1024]{1,0:T(8,128)(2,1)} %param.17) | copy-start | bytes 3145732

commit v4 on v3

--- a/solution.py
+++ b/solution.py
@@ -231,7 +231,7 @@
         )
         for level in range(levels)
     ]
-    for swap in reversed(swaps):
+    for swap in swaps:
         swap.start()
     keep_hidden = pltpu.make_async_copy(hid, hid_out, local_sem.at[6])
     keep_hidden.start()
@@ -239,10 +239,11 @@
     q[...] = dot(normed, wq2[...]).astype(jnp.bfloat16)
     spread(kv2[:rows], turned, ones, kx, vt, 0)
 
-    chunks = [list(range(0, min(3, levels + 1)))]
-    while chunks[-1][-1] < levels:
-        first = chunks[-1][-1] + 1
-        chunks.append(list(range(first, min(first + 2, levels + 1))))
+    chunks, first = [], 0
+    while first <= levels:
+        size = 2 if first + 1 < levels else 1
+        chunks.append(list(range(first, first + size)))
+        first += size
     for chunk in chunks:
         for slot in chunk:
             if slot > 0:

time: 25.7 us -> 25.6 us (level)
  no operation moved by 1% of the time
where the time goes in v4:
time: 25.6 us; the launch traced here: 25.4 us
  Pallas kernels  23 us (90%)
  matrix products  2.36 us (9%)
    pallas_call x1, Pallas kernels, shards(): pl.pallas_call(functools.partial(body, n, levels), name='two_layers', out...  23 us
    dot_general x1, matrix products, shards(): jnp.dot(att, second_out, preferred_element_type=f32) + hidden.astype(f32)  2.36 us

profile of v4, /device:TPU:0, one launch (start us, length us, event | category | flops | bytes accessed | tf_op | source)
XLA Modules:
  0.0 25.4 jit_solution(16535702482614236703)
XLA Ops:
  0.0 0.0 copy-start
  0.0 23.0 %two_layers.1 = (bf16[256,512]{1,0:T(8,128)(2,1)}, bf16[256,1024]{1,0:T(8,128)(2,1)}) custom-call(bf16[256,512]{1,0:T(8,128)(2,1)} %q_hbm.1, bf16[256,256]{1,0:T(8,128)(2,1)} %kv_hbm.1, bf16[256,1024]{1,0:T(8,128)(2,1)} %res_hbm.1, s32[8]{0:T(128)} %extent.1, s32[1,4]{1,0:T(1,128)} %mask.1, bf16[512,1024]{1,0:T(8,128)(2,1)} %wo1_hbm.1, ...), custom_call_target="tpu_custom_call" | custom-call | tf_op jit(solution)/shard_map/two_layers/pallas_call | solution.py:323
  23.0 0.0 copy-done
  23.0 2.4 %fusion = bf16[256,1024]{1,0:T(8,128)(2,1)} fusion(bf16[256,512]{1,0:T(8,128)(2,1)} %get-tuple-element.7, bf16[512,1024]{1,0:T(8,128)(2,1)S(1)} %copy-done, bf16[256,1024]{1,0:T(8,128)(2,1)} %get-tuple-element.8), kind=kOutput, calls=%fused_computation.1 | convolution fusion | flops 269221888 | bytes 2359296 | tf_op jit(solution)/shard_map/dot_general | solution.py:359
Async XLA Ops:
  0.0 23.0 %copy-start = (bf16[512,1024]{1,0:T(8,128)(2,1)S(1)}, bf16[512,1024]{1,0:T(8,128)(2,1)}, u32[]{:S(2)}) copy-start(bf16[512,1024]{1,0:T(8,128)(2,1)} %param.17) | copy-start | bytes 3145732

commit v5 on v4

--- a/solution.py
+++ b/solution.py
@@ -149,11 +149,11 @@
         pair = h // 2
         return q[:, pair * wide : (pair + 1) * wide]
 
-    def put(h, share, halves):
+    def put(h, share, halves, here):
         halves.append(share)
         if h % 2:
             both = jnp.concatenate(halves, axis=0).astype(jnp.bfloat16)
-            att[:, h // 2 * wide : (h // 2 + 1) * wide] = both.T
+            att[here, h // 2 * wide : (h // 2 + 1) * wide] = both.T
             halves.clear()
 
     def own_scores(h):
@@ -189,55 +189,80 @@
     for side in range(2):
         spread(halo[side, :, :wide] * scaled, halo[side, :, wide:].T, ones, kx, vt, 1 + side)
     far = 4 * n * rows
-    left_apart = query - key + rows + jnp.where(has_left, 0, far)
-    right_apart = key - query + rows + jnp.where(has_right, 0, far)
-    halves = []
-
-    def side_scores(h):
-        return [dot_nt(kx[side, h // 2 // per_group, h % 2], queries_of(h)) for side in (1, 2)]
-
-    def side_weigh(h, parts):
-        a = jnp.where(left_apart <= extent[h], parts[0], HIDE)
-        b = jnp.where(right_apart <= extent[h], parts[1], HIDE)
-        before = tops[h, 0:1]
-        top = jnp.maximum(before, col_max([a, b]))
-        return jnp.exp(before - top), weight(a, top), weight(b, top)
-
-    def side_finish(h, fade, a, b):
-        acc = accs[h] * fade
-        acc += dot(vt[1, h // 2 // per_group], a)
-        acc += dot(vt[2, h // 2 // per_group], b)
-        put(h, shared(acc), halves)
-
-    staggered(heads, side_scores, side_weigh, side_finish)
-
-    loads[2].wait()
-    loads[3].wait()
-    hidden = (dot(att[...], wo1[...]) + res[...].astype(jnp.float32)).astype(jnp.bfloat16)
-    hid[...] = hidden
-    values = hidden.astype(jnp.float32)
-    scale = lax.rsqrt(jnp.mean(values * values, axis=-1, keepdims=True) + 1e-05)
-    normed = (values * scale).astype(jnp.bfloat16)
-    loads[4].wait()
-    keyvals = dot(normed, wkv2[...]).astype(jnp.bfloat16)
-    kv2[:rows] = keyvals[:, :wide] * scaled
-    turned = keyvals[:, wide:].T
-    for part in range(rows // wide):
-        kv2[rows + part * wide : rows + (part + 1) * wide] = turned[:, part * wide : (part + 1) * wide]
+    left_off = rows + jnp.where(has_left, 0, far)
+    right_off = rows + jnp.where(has_right, 0, far)
+    tiles = rows // wide
+    for i in (2, 3, 4):
+        loads[i].wait()
     swaps = [
-        pltpu.make_async_remote_copy(
-            kv2, kv2_in.at[level], send_sem.at[2 + level], recv_sem.at[2 + level],
-            device_id={"seq": partner(level)}, device_id_type=MESH,
-        )
+        [
+            pltpu.make_async_remote_copy(
+                kv2.at[pl.ds(tile * 2 * wide, 2 * wide)],
+                kv2_in.at[level, pl.ds(tile * 2 * wide, 2 * wide)],
+                send_sem.at[2 + level * tiles + tile],
+                recv_sem.at[2 + level * tiles + tile],
+                device_id={"seq": partner(level)}, device_id_type=MESH,
+            )
+            for tile in range(tiles)
+        ]
         for level in range(levels)
     ]
-    for swap in swaps:
-        swap.start()
+    halves, normed, turned = [], [], []
+    for tile in range(tiles):
+        here = slice(tile * wide, (tile + 1) * wide)
+        left = slice(tile * wide, rows)
+        right = slice(0, (tile + 1) * wide)
+        left_apart = (query - key)[left, here] + left_off
+        right_apart = (key - query)[right, here] + right_off
+
+        def side_scores(h):
+            pair = h // 2
+            queries = q[here, pair * wide : (pair + 1) * wide]
+            return [
+                dot_nt(kx[1, pair // per_group, h % 2, left], queries),
+                dot_nt(kx[2, pair // per_group, h % 2, right], queries),
+            ]
+
+        def side_weigh(h, parts):
+            a = jnp.where(left_apart <= extent[h], parts[0], HIDE)
+            b = jnp.where(right_apart <= extent[h], parts[1], HIDE)
+            before = tops[h, 0:1, here]
+            top = jnp.maximum(before, col_max([a, b]))
+            return jnp.exp(before - top), weight(a, top), weight(b, top)
+
+        def side_finish(h, fade, a, b):
+            acc = accs[h, :, here] * fade
+            acc += dot(vt[1, h // 2 // per_group, :, left], a)
+            acc += dot(vt[2, h // 2 // per_group, :, right], b)
+            put(h, shared(acc), halves, here)
+
+        staggered(heads, side_scores, side_weigh, side_finish)
+
+        hidden = (dot(att[here], wo1[...]) + res[here].astype(jnp.float32)).astype(jnp.bfloat16)
+        hid[here] = hidden
+        values = hidden.astype(jnp.float32)
+        scale = lax.rsqrt(jnp.mean(values * values, axis=-1, keepdims=True) + 1e-05)
+        normed.append((values * scale).astype(jnp.bfloat16))
+        keyvals = dot(normed[-1], wkv2[...]).astype(jnp.bfloat16)
+        turned.append(keyvals[:, wide:].T)
+        kv2[tile * 2 * wide : (tile * 2 + 1) * wide] = keyvals[:, :wide] * scaled
+        kv2[(tile * 2 + 1) * wide : (tile * 2 + 2) * wide] = turned[-1]
+        for swap in swaps:
+            swap[tile].start()
+
+    def keys_of(block):
+        return jnp.concatenate([block[2 * t * wide : (2 * t + 1) * wide] for t in range(tiles)], axis=0)
+
+    def values_of(block):
+        return jnp.concatenate(
+            [block[(2 * t + 1) * wide : (2 * t + 2) * wide] for t in range(tiles)], axis=1
+        )
+
     keep_hidden = pltpu.make_async_copy(hid, hid_out, local_sem.at[6])
     keep_hidden.start()
     loads[5].wait()
-    q[...] = dot(normed, wq2[...]).astype(jnp.bfloat16)
-    spread(kv2[:rows], turned, ones, kx, vt, 0)
+    q[...] = dot(jnp.concatenate(normed, axis=0), wq2[...]).astype(jnp.bfloat16)
+    spread(keys_of(kv2), values_of(kv2), ones, kx, vt, 0)
 
     chunks, first = [], 0
     while first <= levels:
@@ -247,17 +272,12 @@
     for chunk in chunks:
         for slot in chunk:
             if slot > 0:
-                swaps[slot - 1].wait_recv()
+                for swap in swaps[slot - 1]:
+                    swap.wait_recv()
                 seen = mask[0, slot - 1] == 1
-                came = jnp.concatenate(
-                    [
-                        kv2_in[slot - 1, rows + part * wide : rows + (part + 1) * wide]
-                        for part in range(rows // wide)
-                    ],
-                    axis=1,
-                )
+                came = values_of(kv2_in[slot - 1])
                 spread(
-                    jnp.where(seen, kv2_in[slot - 1, :rows], kv2[:rows]),
+                    jnp.where(seen, keys_of(kv2_in[slot - 1]), keys_of(kv2)),
                     jnp.where(seen, came, jnp.zeros_like(came)),
                     jnp.where(seen, ones, jnp.zeros_like(ones)),
                     kx, vt, slot,
@@ -285,14 +305,15 @@
             if chunk[-1] < levels:
                 accs[h] = acc
             else:
-                put(h, shared(acc), halves)
+                put(h, shared(acc), halves, slice(0, rows))
 
         staggered(heads, far_scores, far_weigh, far_finish)
 
     keep_att = pltpu.make_async_copy(att, att_out, local_sem.at[7])
     keep_att.start()
-    for swap in swaps:
-        swap.wait_send()
+    for level in swaps:
+        for swap in level:
+            swap.wait_send()
 
     @pl.when(has_right)
     def _():
@@ -346,8 +367,8 @@
             pltpu.VMEM((rows, query_width), bf16),
             pltpu.VMEM((rows, width), bf16),
             pltpu.SemaphoreType.DMA((8,)),
-            pltpu.SemaphoreType.DMA((2 + levels,)),
-            pltpu.SemaphoreType.DMA((2 + levels,)),
+            pltpu.SemaphoreType.DMA((2 + levels * (rows // wide),)),
+            pltpu.SemaphoreType.DMA((2 + levels * (rows // wide),)),
         ],
         compiler_params=pltpu.CompilerParams(
             collective_id=0, has_side_effects=True

time: 25.6 us -> 24.1 us (0.941)
  Pallas kernels: 23 us -> 21.5 us
    pallas_call x1, Pallas kernels: 23 us -> 21.5 us  [shards(): pl.pallas_call(functools.partial(body, n, levels), name='two_layers', out...]
where the time goes in v5:
time: 24.1 us; the launch traced here: 23.9 us
  Pallas kernels  21.5 us (89%)
  matrix products  2.36 us (10%)
    pallas_call x1, Pallas kernels, shards(): pl.pallas_call(functools.partial(body, n, levels), name='two_layers', out...  21.5 us
    dot_general x1, matrix products, shards(): jnp.dot(att, second_out, preferred_element_type=f32) + hidden.astype(f32)  2.36 us

profile of v5, /device:TPU:0, one launch (start us, length us, event | category | flops | bytes accessed | tf_op | source)
XLA Modules:
  0.0 23.9 jit_solution(4676791682282340828)
XLA Ops:
  0.0 0.0 copy-start
  0.0 21.5 %two_layers.1 = (bf16[256,512]{1,0:T(8,128)(2,1)}, bf16[256,1024]{1,0:T(8,128)(2,1)}) custom-call(bf16[256,512]{1,0:T(8,128)(2,1)} %q_hbm.1, bf16[256,256]{1,0:T(8,128)(2,1)} %kv_hbm.1, bf16[256,1024]{1,0:T(8,128)(2,1)} %res_hbm.1, s32[8]{0:T(128)} %extent.1, s32[1,4]{1,0:T(1,128)} %mask.1, bf16[512,1024]{1,0:T(8,128)(2,1)} %wo1_hbm.1, ...), custom_call_target="tpu_custom_call" | custom-call | tf_op jit(solution)/shard_map/two_layers/pallas_call | solution.py:344
  21.6 0.0 copy-done
  21.6 2.4 %fusion = bf16[256,1024]{1,0:T(8,128)(2,1)} fusion(bf16[256,512]{1,0:T(8,128)(2,1)} %get-tuple-element.7, bf16[512,1024]{1,0:T(8,128)(2,1)S(1)} %copy-done, bf16[256,1024]{1,0:T(8,128)(2,1)} %get-tuple-element.8), kind=kOutput, calls=%fused_computation.1 | convolution fusion | flops 269221888 | bytes 2359296 | tf_op jit(solution)/shard_map/dot_general | solution.py:380
Async XLA Ops:
  0.0 21.6 %copy-start = (bf16[512,1024]{1,0:T(8,128)(2,1)S(1)}, bf16[512,1024]{1,0:T(8,128)(2,1)}, u32[]{:S(2)}) copy-start(bf16[512,1024]{1,0:T(8,128)(2,1)} %param.17) | copy-start | bytes 3145732

commit v6 on v5

--- a/solution.py
+++ b/solution.py
@@ -27,17 +27,17 @@
     return jnp.concatenate([x[:, HEAD_SIZE:], x[:, :HEAD_SIZE]], axis=1)
 
 
-def spread(keys, values, ones, kx, vt, slot):
+def spread(keys, values, ones, kx, vt, slot, part=slice(None)):
     low = lax.broadcasted_iota(jnp.int32, keys.shape, 1) < HEAD_SIZE
     none = jnp.zeros_like(keys)
     first, second = jnp.where(low, keys, none), jnp.where(low, none, keys)
-    kx[slot, 0, 0] = first
-    kx[slot, 0, 1] = rolled(first)
-    kx[slot, 1, 0] = rolled(second)
-    kx[slot, 1, 1] = second
+    kx[slot, 0, 0, part] = first
+    kx[slot, 0, 1, part] = rolled(first)
+    kx[slot, 1, 0, part] = rolled(second)
+    kx[slot, 1, 1, part] = second
     for group in range(2):
-        vt[slot, group, :HEAD_SIZE] = values[group * HEAD_SIZE : (group + 1) * HEAD_SIZE]
-        vt[slot, group, HEAD_SIZE:] = ones
+        vt[slot, group, :HEAD_SIZE, part] = values[group * HEAD_SIZE : (group + 1) * HEAD_SIZE]
+        vt[slot, group, HEAD_SIZE:, part] = ones
 
 
 def col_max(parts):
@@ -264,45 +264,56 @@
     q[...] = dot(jnp.concatenate(normed, axis=0), wq2[...]).astype(jnp.bfloat16)
     spread(keys_of(kv2), values_of(kv2), ones, kx, vt, 0)
 
+    blocks = [[(slot, tile) for tile in range(tiles)] for slot in range(levels + 1)]
     chunks, first = [], 0
     while first <= levels:
         size = 2 if first + 1 < levels else 1
-        chunks.append(list(range(first, first + size)))
+        chunks.append(sum(blocks[first : first + size], []))
         first += size
+    if len(chunks) > 1:
+        chunks[-2] += chunks[-1][:-1]
+        chunks[-1] = chunks[-1][-1:]
     for chunk in chunks:
-        for slot in chunk:
+        final = chunk is chunks[-1]
+        for slot, tile in chunk:
             if slot > 0:
-                for swap in swaps[slot - 1]:
-                    swap.wait_recv()
+                swaps[slot - 1][tile].wait_recv()
                 seen = mask[0, slot - 1] == 1
-                came = values_of(kv2_in[slot - 1])
+                here = slice(tile * wide, (tile + 1) * wide)
+                at = slice(2 * tile * wide, (2 * tile + 1) * wide)
+                came = kv2_in[slot - 1, (2 * tile + 1) * wide : (2 * tile + 2) * wide]
+                total = ones[:, :wide]
                 spread(
-                    jnp.where(seen, keys_of(kv2_in[slot - 1]), keys_of(kv2)),
+                    jnp.where(seen, kv2_in[slot - 1, at], kv2[at]),
                     jnp.where(seen, came, jnp.zeros_like(came)),
-                    jnp.where(seen, ones, jnp.zeros_like(ones)),
-                    kx, vt, slot,
+                    jnp.where(seen, total, jnp.zeros_like(total)),
+                    kx, vt, slot, here,
                 )
+        spans = []
+        for slot in dict.fromkeys(slot for slot, tile in chunk):
+            held = [tile for at, tile in chunk if at == slot]
+            spans.append((slot, slice(held[0] * wide, (held[-1] + 1) * wide)))
 
         def far_scores(h):
-            return [dot_nt(kx[slot, h // 2 // per_group, h % 2], queries_of(h)) for slot in chunk]
+            return [dot_nt(kx[slot, h // 2 // per_group, h % 2, span], queries_of(h)) for slot, span in spans]
 
         def far_weigh(h, parts):
             top = col_max(parts)
             fade = None
-            if chunk[0] > 0:
+            if chunk is not chunks[0]:
                 before = tops[h, 0:1]
                 top = jnp.maximum(before, top)
                 fade = jnp.exp(before - top)
-            if chunk[-1] < levels:
+            if not final:
                 tops[h] = jnp.broadcast_to(top, tops.shape[1:])
             return fade, [weight(part, top) for part in parts]
 
         def far_finish(h, fade, parts):
             acc = None if fade is None else accs[h] * fade
-            for slot, part in zip(chunk, parts):
-                term = dot(vt[slot, h // 2 // per_group], part)
+            for (slot, span), part in zip(spans, parts):
+                term = dot(vt[slot, h // 2 // per_group, :, span], part)
                 acc = term if acc is None else acc + term
-            if chunk[-1] < levels:
+            if not final:
                 accs[h] = acc
             else:
                 put(h, shared(acc), halves, slice(0, rows))

time: 24.1 us -> 24.2 us (level)
  no operation moved by 1% of the time
where the time goes in v6:
time: 24.2 us; the launch traced here: 24.1 us
  Pallas kernels  21.7 us (90%)
  matrix products  2.36 us (10%)
    pallas_call x1, Pallas kernels, shards(): pl.pallas_call(functools.partial(body, n, levels), name='two_layers', out...  21.7 us
    dot_general x1, matrix products, shards(): jnp.dot(att, second_out, preferred_element_type=f32) + hidden.astype(f32)  2.36 us

profile of v6, /device:TPU:0, one launch (start us, length us, event | category | flops | bytes accessed | tf_op | source)
XLA Modules:
  0.0 24.1 jit_solution(7160609859608521260)
XLA Ops:
  0.0 0.0 copy-start
  0.0 21.7 %two_layers.1 = (bf16[256,512]{1,0:T(8,128)(2,1)}, bf16[256,1024]{1,0:T(8,128)(2,1)}) custom-call(bf16[256,512]{1,0:T(8,128)(2,1)} %q_hbm.1, bf16[256,256]{1,0:T(8,128)(2,1)} %kv_hbm.1, bf16[256,1024]{1,0:T(8,128)(2,1)} %res_hbm.1, s32[8]{0:T(128)} %extent.1, s32[1,4]{1,0:T(1,128)} %mask.1, bf16[512,1024]{1,0:T(8,128)(2,1)} %wo1_hbm.1, ...), custom_call_target="tpu_custom_call" | custom-call | tf_op jit(solution)/shard_map/two_layers/pallas_call | solution.py:355
  21.7 0.0 copy-done
  21.7 2.4 %fusion = bf16[256,1024]{1,0:T(8,128)(2,1)} fusion(bf16[256,512]{1,0:T(8,128)(2,1)} %get-tuple-element.7, bf16[512,1024]{1,0:T(8,128)(2,1)S(1)} %copy-done, bf16[256,1024]{1,0:T(8,128)(2,1)} %get-tuple-element.8), kind=kOutput, calls=%fused_computation.1 | convolution fusion | flops 269221888 | bytes 2359296 | tf_op jit(solution)/shard_map/dot_general | solution.py:391
Async XLA Ops:
  0.0 21.7 %copy-start = (bf16[512,1024]{1,0:T(8,128)(2,1)S(1)}, bf16[512,1024]{1,0:T(8,128)(2,1)}, u32[]{:S(2)}) copy-start(bf16[512,1024]{1,0:T(8,128)(2,1)} %param.17) | copy-start | bytes 3145732
